TPU v7x, 32 devices: a whole 2x2x4 slice. The times are simulated.
32 devices in a mesh: pair: 8 (over y, x, core), aux: 4 (over z).
Axes of the slice: x: 2, y: 2, z: 4, core: 2. Of those that a mesh axis runs over, the one named last changes fastest.
Arguments:
- three_center: float32 [2048, 8192], P('aux', 'pair'), may hold values from -0.0625 to 0.0625
- densities: float32 [8192, 512], P(('pair', 'aux')), may hold values from -6 to 6
- screen_mask: int32 [32, 128], P('aux', 'pair'), may hold values 0 or 1
- diag_inverse: float32 [2048, 512], P('aux'), as said below
- sub_factor: float32 [2048, 512], P('aux'), as said below
Outputs:
- response: float32 [8192, 512], P(('pair', 'aux'))
Inputs may be any that keep to these rules, and one draw needn't show every extreme that they name: `diag_inverse`: each block of 512 rows is lower triangular; its diagonal lies in 0.75 to 1.3 and its entries below the diagonal within plus or minus 2 / sqrt(512). `sub_factor`: block 0 is not used; entries lie within plus or minus 3.4 / sqrt(512).
All inputs are finite; a program needn't handle non-finite values. No bound on the sum of `screen_mask` on one device may be relied on, other than what follows from the above.
Results may differ from a plain program's by a relative error of at most 0.0003.
Values sent between devices are 32-bit elements; how exact they have to be, the bound alone decides.
No kernel may reach another device: no remote copies, remote signals or barrier semaphores. Data moves between devices by JAX's collectives and lax.ppermute only.
A program may use at most 192 MiB of HBM per device.

v0:
```python
import jax
import jax.numpy as jnp
from jax import lax
from jax.sharding import PartitionSpec as P


def from_behind(array, axis, by):
    count = lax.axis_size(axis)
    pairs = [(i, i + by) for i in range(count) if 0 <= i + by < count]
    return lax.ppermute(array, axis, pairs)


def screen_block(block, screen_mask):
    aux_blocks, pair_blocks = screen_mask.shape
    aux_size = block.shape[0] // aux_blocks
    pair_size = block.shape[1] // pair_blocks
    shaped = block.reshape(aux_blocks, aux_size, pair_blocks, pair_size)
    shaped = shaped * screen_mask.astype(jnp.float32)[:, None, :, None]
    return shaped.reshape(block.shape)


def product(left, right):
    return jnp.dot(left, right, precision=lax.Precision.HIGHEST, preferred_element_type=jnp.float32)


def contract_first(left, right):
    return lax.dot_general(
        left,
        right,
        (((0,), (0,)), ((), ())),
        precision=lax.Precision.HIGHEST,
        preferred_element_type=jnp.float32,
    )


def per_device(three_center, densities, screen_mask, diag_inverse, sub_factor):
    screened = screen_block(three_center, screen_mask)
    dens_full = lax.all_gather(densities, "aux", axis=0, tiled=True)
    gamma_share = lax.psum_scatter(
        contract_first(dens_full, screened.T), "pair", scatter_dimension=0, tiled=True
    )
    right_side = gamma_share.T
    transfer = -product(diag_inverse, sub_factor)
    driving = product(diag_inverse, right_side)
    chain_length = lax.axis_size("aux")

    def forward(turn_index, incoming):
        return from_behind(product(transfer, incoming) + driving, "aux", 1)

    incoming = lax.fori_loop(0, chain_length - 1, forward, jnp.zeros_like(driving))
    solved = product(transfer, incoming) + driving
    source = product(sub_factor.T, product(diag_inverse.T, solved))
    back_map = transfer.T

    def backward(turn_index, arriving):
        return from_behind(product(back_map, arriving) + source, "aux", -1)

    arriving = lax.fori_loop(0, chain_length - 1, backward, jnp.zeros_like(driving))
    coefficients = product(diag_inverse.T, solved - arriving)
    coeff_full = lax.all_gather(coefficients, "pair", axis=1, tiled=True)
    return lax.psum_scatter(
        contract_first(screened, coeff_full), "aux", scatter_dimension=0, tiled=True
    )


def solution(mesh):
    return jax.shard_map(
        per_device,
        mesh=mesh,
        in_specs=(
            P("aux", "pair"),
            P(("pair", "aux"), None),
            P("aux", "pair"),
            P("aux", None),
            P("aux", None),
        ),
        out_specs=P(("pair", "aux"), None),
        check_vma=False,
    )
```

profile of v0, /device:TPU:0, one launch (start us, length us, event | category | flops | bytes accessed | tf_op | source)
XLA Modules:
  0.0 238.7 jit_solution(8295645147686337585)
XLA Ops:
  8.0 2.3 mul.11
  10.3 4.9 %mul.12 = f32[512,1024]{1,0:T(8,128)} reshape(f32[8,64,16,64]{3,2,1,0:T(8,128)} %mul.11) | data formatting | bytes 4194304 | tf_op jit(solution)/shard_map/mul | solution.py:18
  15.2 2.6 %mul.13 = f32[512,1024]{1,0:T(8,128)S(1)} multiply(f32[512,1024]{1,0:T(8,128)} %param.9, f32[512,1024]{1,0:T(8,128)} %mul.12) | non-fusion elementwise | flops 524288 | bytes 6291456 | tf_op jit(solution)/shard_map/mul | solution.py:18
  17.8 39.8 %all-gather.3.cloned.1.call-done = f32[1024,512]{1,0:T(8,128)} async-done(((f32[256,512]{1,0:T(8,128)}), f32[1024,512]{1,0:T(8,128)}) %all-gather.3.cloned.1.call-update) | async-done | bytes 2097168 | tf_op jit(solution)/shard_map/all_gather | solution.py:38
  57.6 6.1 %convolution_bitcast_fusion = f32[512,512]{0,1:T(8,128)} fusion(f32[512,1024]{1,0:T(8,128)S(1)} %mul.13, f32[1024,512]{1,0:T(8,128)} %all-gather.3.cloned.1.call-done), kind=kOutput, calls=%fused_computation.2 | convolution fusion | flops 3221225472 | bytes 5242880 | tf_op jit(solution)/shard_map/dot_general | solution.py:27
  63.7 2.5 %copy.8 = f32[512,512]{1,0:T(8,128)} copy(f32[512,512]{0,1:T(8,128)} %convolution_bitcast_fusion) | data formatting | bytes 2097152
  66.5 3.1 %convolution_negate_fusion = f32[512,512]{1,0:T(8,128)S(1)} fusion(f32[512,512]{1,0:T(8,128)S(1)} %copy-done, f32[512,512]{1,0:T(8,128)} %param.13), kind=kOutput, calls=%fused_computation.3 | convolution fusion | flops 1610874880 | bytes 3145728 | tf_op jit(solution)/shard_map/dot_general | solution.py:23
  69.9 31.3 %reduce-scatter.7.cloned.1.call-done = f32[64,512]{1,0:T(8,128)} async-done(((f32[512,512]{1,0:T(8,128)}), f32[64,512]{1,0:T(8,128)}) %reduce-scatter.7.cloned.1.call-update) | async-done | bytes 131088
  101.2 2.0 convolution_bitcast_fusion.3
  103.2 23.2 %while.20 = (s32[]{:T(128)}, f32[512,64]{0,1:T(8,128)S(1)}, f32[512,512]{1,0:T(8,128)S(1)}, f32[512,64]{0,1:T(8,128)S(1)}, s32[]{:T(128)}) while((s32[]{:T(128)}, f32[512,64]{0,1:T(8,128)S(1)}, f32[512,512]{1,0:T(8,128)S(1)}, f32[512,64]{0,1:T(8,128)S(1)}, s32[]{:T(128)}) %tuple.33), condition=%wide.region_2.0_spmd, body=%wide.region_1.0_spmd.sunk | while | flops 201359360 | bytes 1966181 | solution.py:50
  104.4 3.4 %collective-permute-start = (f32[512,64]{0,1:T(8,128)S(1)}, f32[512,64]{0,1:T(8,128)S(1)}, u32[]{:S(2)}, u32[]{:S(2)}) collective-permute-start(f32[512,64]{0,1:T(8,128)S(1)} %convolution_add_fusion.5), channel_id=1, source_target_pairs={{0,1},{1,2},{2,3},{4,5},{5,6},{6,7},{8,9},{9,10},{10,11},{12,13},{... | collective-permute-start | bytes 393224 | tf_op jit(solution)/shard_map/while/body/eval_jaxpr/ppermute | solution.py:10
  107.8 2.6 %collective-permute-done = f32[512,64]{0,1:T(8,128)S(1)} collective-permute-done((f32[512,64]{0,1:T(8,128)S(1)}, f32[512,64]{0,1:T(8,128)S(1)}, u32[]{:S(2)}, u32[]{:S(2)}) %collective-permute-start) | collective-permute-done | bytes 131104 | tf_op jit(solution)/shard_map/while/body/eval_jaxpr/ppermute | solution.py:10
  111.5 4.4 %collective-permute-start = (f32[512,64]{0,1:T(8,128)S(1)}, f32[512,64]{0,1:T(8,128)S(1)}, u32[]{:S(2)}, u32[]{:S(2)}) collective-permute-start(f32[512,64]{0,1:T(8,128)S(1)} %convolution_add_fusion.5), channel_id=1, source_target_pairs={{0,1},{1,2},{2,3},{4,5},{5,6},{6,7},{8,9},{9,10},{10,11},{12,13},{... | collective-permute-start | bytes 393224 | tf_op jit(solution)/shard_map/while/body/eval_jaxpr/ppermute | solution.py:10
  115.9 2.5 %collective-permute-done = f32[512,64]{0,1:T(8,128)S(1)} collective-permute-done((f32[512,64]{0,1:T(8,128)S(1)}, f32[512,64]{0,1:T(8,128)S(1)}, u32[]{:S(2)}, u32[]{:S(2)}) %collective-permute-start) | collective-permute-done | bytes 131104 | tf_op jit(solution)/shard_map/while/body/eval_jaxpr/ppermute | solution.py:10
  119.5 4.4 %collective-permute-start = (f32[512,64]{0,1:T(8,128)S(1)}, f32[512,64]{0,1:T(8,128)S(1)}, u32[]{:S(2)}, u32[]{:S(2)}) collective-permute-start(f32[512,64]{0,1:T(8,128)S(1)} %convolution_add_fusion.5), channel_id=1, source_target_pairs={{0,1},{1,2},{2,3},{4,5},{5,6},{6,7},{8,9},{9,10},{10,11},{12,13},{... | collective-permute-start | bytes 393224 | tf_op jit(solution)/shard_map/while/body/eval_jaxpr/ppermute | solution.py:10
  123.9 2.5 %collective-permute-done = f32[512,64]{0,1:T(8,128)S(1)} collective-permute-done((f32[512,64]{0,1:T(8,128)S(1)}, f32[512,64]{0,1:T(8,128)S(1)}, u32[]{:S(2)}, u32[]{:S(2)}) %collective-permute-start) | collective-permute-done | bytes 131104 | tf_op jit(solution)/shard_map/while/body/eval_jaxpr/ppermute | solution.py:10
  129.1 24.6 %while.21 = (s32[]{:T(128)}, f32[512,64]{0,1:T(8,128)S(1)}, f32[512,512]{1,0:T(8,128)S(1)}, f32[512,64]{0,1:T(8,128)S(1)}, s32[]{:T(128)}) while((s32[]{:T(128)}, f32[512,64]{0,1:T(8,128)S(1)}, f32[512,512]{1,0:T(8,128)S(1)}, f32[512,64]{0,1:T(8,128)S(1)}, s32[]{:T(128)}) %tuple.36), condition=%wide.region_4.0_spmd, body=%wide.region_3.0_spmd.sunk | while | flops 201359360 | bytes 1966181 | solution.py:58
  131.5 6.0 %collective-permute-done.1 = f32[512,64]{0,1:T(8,128)S(1)} collective-permute-done((f32[512,64]{0,1:T(8,128)S(1)}, f32[512,64]{0,1:T(8,128)S(1)}, u32[]{:S(2)}, u32[]{:S(2)}) %collective-permute-start.1) | collective-permute-done | bytes 131104 | tf_op jit(solution)/shard_map/while/body/eval_jaxpr/ppermute | solution.py:10
  140.0 5.6 %collective-permute-done.1 = f32[512,64]{0,1:T(8,128)S(1)} collective-permute-done((f32[512,64]{0,1:T(8,128)S(1)}, f32[512,64]{0,1:T(8,128)S(1)}, u32[]{:S(2)}, u32[]{:S(2)}) %collective-permute-start.1) | collective-permute-done | bytes 131104 | tf_op jit(solution)/shard_map/while/body/eval_jaxpr/ppermute | solution.py:10
  148.0 5.7 %collective-permute-done.1 = f32[512,64]{0,1:T(8,128)S(1)} collective-permute-done((f32[512,64]{0,1:T(8,128)S(1)}, f32[512,64]{0,1:T(8,128)S(1)}, u32[]{:S(2)}, u32[]{:S(2)}) %collective-permute-start.1) | collective-permute-done | bytes 131104 | tf_op jit(solution)/shard_map/while/body/eval_jaxpr/ppermute | solution.py:10
  153.6 1.4 convolution_bitcast_fusion.1
  155.3 23.0 %all-gather.5.cloned.1.call-done = f32[512,512]{0,1:T(8,128)} async-done(((f32[512,64]{0,1:T(8,128)}), f32[512,512]{0,1:T(8,128)}) %all-gather.5.cloned.1.call-update) | async-done | bytes 1048592 | tf_op jit(solution)/shard_map/all_gather | solution.py:60
  178.3 9.8 %fusion.2 = f32[1024,512]{1,0:T(8,128)} fusion(f32[512,1024]{1,0:T(8,128)} %copy-done.1, f32[512,512]{0,1:T(8,128)} %all-gather.5.cloned.1.call-done), kind=kOutput, calls=%fused_computation.10 | convolution fusion | flops 3221225472 | bytes 5242880 | tf_op jit(solution)/shard_map/dot_general | solution.py:27
  188.2 44.0 %reduce-scatter.5.cloned.1.call-done = f32[256,512]{1,0:T(8,128)} async-done(((f32[1024,512]{1,0:T(8,128)}), f32[256,512]{1,0:T(8,128)}) %reduce-scatter.5.cloned.1.call-update) | async-done | bytes 524304 | tf_op jit(solution)/shard_map/reduce_scatter | solution.py:61
  (30 shorter events, 15.7 us)
Async XLA Ops:
  6.5 59.9 %copy-start = (f32[512,512]{1,0:T(8,128)S(1)}, f32[512,512]{1,0:T(8,128)}, u32[]{:S(2)}) copy-start(f32[512,512]{1,0:T(8,128)} %param.12) | copy-start | bytes 3145732
  6.5 51.1 %all-gather.3.cloned.1.call-start = ((), (), s32[]{:S(2)}) async-start(), calls=%async_computation.2 | async-start | bytes 2621440 | tf_op jit(solution)/shard_map/all_gather | solution.py:38
  7.3 93.9 %reduce-scatter.7.cloned.1.call-start = ((), (), s32[]{:S(2)}) async-start(), calls=%async_computation.5 | async-start | bytes 1179648
  17.8 45.9 %copy-start.1 = (f32[512,1024]{1,0:T(8,128)}, f32[512,1024]{1,0:T(8,128)S(1)}, u32[]{:S(2)}) copy-start(f32[512,1024]{1,0:T(8,128)S(1)} %mul.13) | copy-start | bytes 6291460
  66.3 112.1 %all-gather.5.cloned.1.call-start = ((), (), s32[]{:S(2)}) async-start(), calls=%async_computation.3 | async-start | bytes 1179648 | tf_op jit(solution)/shard_map/all_gather | solution.py:60
  104.4 6.0 %collective-permute-start = (f32[512,64]{0,1:T(8,128)S(1)}, f32[512,64]{0,1:T(8,128)S(1)}, u32[]{:S(2)}, u32[]{:S(2)}) collective-permute-start(f32[512,64]{0,1:T(8,128)S(1)} %convolution_add_fusion.5), channel_id=1, source_target_pairs={{0,1},{1,2},{2,3},{4,5},{5,6},{6,7},{8,9},{9,10},{10,11},{12,13},{... | collective-permute-start | bytes 393224 | tf_op jit(solution)/shard_map/while/body/eval_jaxpr/ppermute | solution.py:10
  111.5 6.9 %collective-permute-start = (f32[512,64]{0,1:T(8,128)S(1)}, f32[512,64]{0,1:T(8,128)S(1)}, u32[]{:S(2)}, u32[]{:S(2)}) collective-permute-start(f32[512,64]{0,1:T(8,128)S(1)} %convolution_add_fusion.5), channel_id=1, source_target_pairs={{0,1},{1,2},{2,3},{4,5},{5,6},{6,7},{8,9},{9,10},{10,11},{12,13},{... | collective-permute-start | bytes 393224 | tf_op jit(solution)/shard_map/while/body/eval_jaxpr/ppermute | solution.py:10
  119.5 6.9 %collective-permute-start = (f32[512,64]{0,1:T(8,128)S(1)}, f32[512,64]{0,1:T(8,128)S(1)}, u32[]{:S(2)}, u32[]{:S(2)}) collective-permute-start(f32[512,64]{0,1:T(8,128)S(1)} %convolution_add_fusion.5), channel_id=1, source_target_pairs={{0,1},{1,2},{2,3},{4,5},{5,6},{6,7},{8,9},{9,10},{10,11},{12,13},{... | collective-permute-start | bytes 393224 | tf_op jit(solution)/shard_map/while/body/eval_jaxpr/ppermute | solution.py:10
  126.4 1.9 copy-start.2
  130.2 7.3 %collective-permute-start.1 = (f32[512,64]{0,1:T(8,128)S(1)}, f32[512,64]{0,1:T(8,128)S(1)}, u32[]{:S(2)}, u32[]{:S(2)}) collective-permute-start(f32[512,64]{0,1:T(8,128)S(1)} %convolution_add_fusion.6), channel_id=1, source_target_pairs={{1,0},{2,1},{3,2},{5,4},{6,5},{7,6},{9,8},{10,9},{11,10},{13,12},{... | collective-permute-start | bytes 393224 | tf_op jit(solution)/shard_map/while/body/eval_jaxpr/ppermute | solution.py:10
  138.7 6.9 %collective-permute-start.1 = (f32[512,64]{0,1:T(8,128)S(1)}, f32[512,64]{0,1:T(8,128)S(1)}, u32[]{:S(2)}, u32[]{:S(2)}) collective-permute-start(f32[512,64]{0,1:T(8,128)S(1)} %convolution_add_fusion.6), channel_id=1, source_target_pairs={{1,0},{2,1},{3,2},{5,4},{6,5},{7,6},{9,8},{10,9},{11,10},{13,12},{... | collective-permute-start | bytes 393224 | tf_op jit(solution)/shard_map/while/body/eval_jaxpr/ppermute | solution.py:10
  146.7 7.0 %collective-permute-start.1 = (f32[512,64]{0,1:T(8,128)S(1)}, f32[512,64]{0,1:T(8,128)S(1)}, u32[]{:S(2)}, u32[]{:S(2)}) collective-permute-start(f32[512,64]{0,1:T(8,128)S(1)} %convolution_add_fusion.6), channel_id=1, source_target_pairs={{1,0},{2,1},{3,2},{5,4},{6,5},{7,6},{9,8},{10,9},{11,10},{13,12},{... | collective-permute-start | bytes 393224 | tf_op jit(solution)/shard_map/while/body/eval_jaxpr/ppermute | solution.py:10
  155.1 77.1 %reduce-scatter.5.cloned.1.call-start = ((), (), s32[]{:S(2)}) async-start(), calls=%async_computation.4 | async-start | bytes 2621440 | tf_op jit(solution)/shard_map/reduce_scatter | solution.py:61
Sparse Core Ops, SparseCore 0:
  8.9 48.6 all-gather.2
  66.4 34.7 reduce-scatter.6
  155.2 23.0 all-gather.4
  188.3 43.8 reduce-scatter.4
where the time goes:
time: 239 us
  waiting for transfers between devices  164 us (69%)
  matrix products  31.9 us (13%)
  starting transfers between devices  16.5 us (7%)
  between operations  13.2 us (6%)
  local copies, waits for them, and re-layouts  10.1 us (4%)
  other arithmetic  3.3 us (1%)
    reduce_scatter x1, waiting for transfers between devices, per_device(): lax.psum_scatter(contract_first(screened, coeff_full), 'aux', scatter_dim...  44 us
    all_gather x1, waiting for transfers between devices, per_device(): dens_full = lax.all_gather(densities, 'aux', axis=0, tiled=True)  39.8 us
    unnamed x5, waiting for transfers between devices  32 us
    ppermute x6, waiting for transfers between devices, from_behind(): return lax.ppermute(array, axis, pairs)  24.8 us
    all_gather x1, waiting for transfers between devices, per_device(): coeff_full = lax.all_gather(coefficients, 'pair', axis=1, tiled=True)  23 us
    ppermute x6, starting transfers between devices, from_behind(): return lax.ppermute(array, axis, pairs)  16 us
    dot_general x12, matrix products, product(): jnp.dot(left, right, precision=lax.Precision.HIGHEST, preferred_element_t...  16 us
    dot_general x2, matrix products, contract_first(): lax.dot_general(left, right, (((0,), (0,)), ((), ())), precision=lax.Prec...  15.9 us
  transfers between devices with their start and end apart: 10, of which 10 were waited for; matrix products, arithmetic and copies ran while one was open for 6% of the time, Pallas kernels for 0%

commit v1 on v0

--- a/solution.py
+++ b/solution.py
@@ -57,7 +57,24 @@
 
     arriving = lax.fori_loop(0, chain_length - 1, backward, jnp.zeros_like(driving))
     coefficients = product(diag_inverse.T, solved - arriving)
-    coeff_full = lax.all_gather(coefficients, "pair", axis=1, tiled=True)
+    z = lax.axis_size("pair")
+    y2 = lax.axis_index("pair")
+    spare, res, all_rows = (z, y2, coefficients.shape[1])
+    seen = [nth * spare if d == 1 else nth for d, nth in enumerate(coefficients.shape)]
+    coeff_full = lax.dynamic_update_slice_in_dim(
+        jnp.zeros(seen, coefficients.dtype), coefficients, res * all_rows, axis=1
+    )
+    q_next = w2 = coefficients
+    for q in tuple(range(1, spare // 2 + 1)):
+        q_next = lax.ppermute(q_next, "pair", [(d, (d + 1) % spare) for d in range(spare)])
+        coeff_full = lax.dynamic_update_slice_in_dim(
+            coeff_full, q_next, (res - q) % spare * all_rows, axis=1
+        )
+        if 2 * q < spare:
+            w2 = lax.ppermute(w2, "pair", [(d, (d - 1) % spare) for d in range(spare)])
+            coeff_full = lax.dynamic_update_slice_in_dim(
+                coeff_full, w2, (res + q) % spare * all_rows, axis=1
+            )
     return lax.psum_scatter(
         contract_first(screened, coeff_full), "aux", scatter_dimension=0, tiled=True
     )

time: 239 us -> 240 us (level)
  waiting for transfers between devices: 164 us -> 152 us
  starting transfers between devices: 16.5 us -> 24.2 us
  local copies, waits for them, and re-layouts: 10.1 us -> 15.8 us
    all_gather x1 -> x0, waiting for transfers between devices: 23 us -> none  [per_device(): coeff_full = lax.all_gather(coefficients, 'pair', axis=1, tiled=True)]
    ppermute x0 -> x7, waiting for transfers between devices: none -> 12 us  [the longest x4 12 us: per_device(): lax.ppermute(q_next, 'pair', [(d, (d + 1) % spare) for d in range(spare)])]
    ppermute x0 -> x7, starting transfers between devices: none -> 7.94 us  [the longest x3 7.93 us: per_device(): w2 = lax.ppermute(w2, 'pair', [(d, (d - 1) % spare) for d in range(spare)])]
    dynamic_update_slice x0 -> x7, local copies, waits for them, and re-layouts: none -> 4.64 us  [the longest x4 2.66 us: per_device(): lax.dynamic_update_slice_in_dim(coeff_full, q_next, (res - q) % spare * a...]
    unnamed x5 -> x4, waiting for transfers between devices: 32 us -> 32 us
  transfers between devices with their start and end apart: 10 -> 16, of which waited for: 10 -> 13; matrix products, arithmetic and copies ran while one was open for 6% -> 8% of each run, Pallas kernels for 0% -> 0%
where the time goes in v1:
time: 240 us; the launch traced here: 239 us
  waiting for transfers between devices  152 us (63%)
  matrix products  30.6 us (13%)
  starting transfers between devices  24.2 us (10%)
  local copies, waits for them, and re-layouts  15.8 us (7%)
  between operations  13.2 us (6%)
  other arithmetic  3.46 us (1%)
    reduce_scatter x1, waiting for transfers between devices, per_device(): lax.psum_scatter(contract_first(screened, coeff_full), 'aux', scatter_dim...  43.4 us
    all_gather x1, waiting for transfers between devices, per_device(): dens_full = lax.all_gather(densities, 'aux', axis=0, tiled=True)  39.6 us
    unnamed x4, waiting for transfers between devices  32 us
    ppermute x6, waiting for transfers between devices, from_behind(): return lax.ppermute(array, axis, pairs)  24.8 us
    ppermute x6, starting transfers between devices, from_behind(): return lax.ppermute(array, axis, pairs)  16 us
    dot_general x12, matrix products, product(): jnp.dot(left, right, precision=lax.Precision.HIGHEST, preferred_element_t...  15.3 us
    dot_general x2, matrix products, contract_first(): lax.dot_general(left, right, (((0,), (0,)), ((), ())), precision=lax.Prec...  15.3 us
    ppermute x4, waiting for transfers between devices, per_device(): lax.ppermute(q_next, 'pair', [(d, (d + 1) % spare) for d in range(spare)])  12 us
  transfers between devices with their start and end apart: 16, of which 13 were waited for; matrix products, arithmetic and copies ran while one was open for 8% of the time, Pallas kernels for 0%

profile of v1, /device:TPU:0, one launch (start us, length us, event | category | flops | bytes accessed | tf_op | source)
XLA Modules:
  0.0 239.3 jit_solution(17261781224401961737)
XLA Ops:
  10.3 4.9 %mul.36 = f32[512,1024]{1,0:T(8,128)} reshape(f32[8,64,16,64]{3,2,1,0:T(8,128)} %mul.35) | data formatting | bytes 4194304 | tf_op jit(solution)/shard_map/mul | solution.py:18
  15.2 2.8 %mul.37 = f32[512,1024]{1,0:T(8,128)S(1)} multiply(f32[512,1024]{1,0:T(8,128)} %param.9, f32[512,1024]{1,0:T(8,128)} %mul.36) | non-fusion elementwise | flops 524288 | bytes 6291456 | tf_op jit(solution)/shard_map/mul | solution.py:18
  18.0 39.6 %all-gather.2.cloned.1.call-done = f32[1024,512]{1,0:T(8,128)} async-done(((f32[256,512]{1,0:T(8,128)}), f32[1024,512]{1,0:T(8,128)}) %all-gather.2.cloned.1.call-update) | async-done | bytes 2097168 | tf_op jit(solution)/shard_map/all_gather | solution.py:38
  57.6 6.1 %convolution_bitcast_fusion = f32[512,512]{0,1:T(8,128)} fusion(f32[512,1024]{1,0:T(8,128)S(1)} %mul.37, f32[1024,512]{1,0:T(8,128)} %all-gather.2.cloned.1.call-done), kind=kOutput, calls=%fused_computation.2 | convolution fusion | flops 3221225472 | bytes 5242880 | tf_op jit(solution)/shard_map/dot_general | solution.py:27
  63.7 2.5 %copy.8 = f32[512,512]{1,0:T(8,128)} copy(f32[512,512]{0,1:T(8,128)} %convolution_bitcast_fusion) | data formatting | bytes 2097152
  66.5 3.1 %convolution_negate_fusion = f32[512,512]{1,0:T(8,128)S(1)} fusion(f32[512,512]{1,0:T(8,128)S(1)} %copy-done, f32[512,512]{1,0:T(8,128)} %param.13), kind=kOutput, calls=%fused_computation.3 | convolution fusion | flops 1610874880 | bytes 3145728 | tf_op jit(solution)/shard_map/dot_general | solution.py:23
  69.9 31.3 %reduce-scatter.7.cloned.1.call-done = f32[64,512]{1,0:T(8,128)} async-done(((f32[512,512]{1,0:T(8,128)}), f32[64,512]{1,0:T(8,128)}) %reduce-scatter.7.cloned.1.call-update) | async-done | bytes 131088
  103.2 23.2 %while.20 = (s32[]{:T(128)}, f32[512,64]{0,1:T(8,128)S(1)}, f32[512,512]{1,0:T(8,128)S(1)}, f32[512,64]{0,1:T(8,128)S(1)}, s32[]{:T(128)}) while((s32[]{:T(128)}, f32[512,64]{0,1:T(8,128)S(1)}, f32[512,512]{1,0:T(8,128)S(1)}, f32[512,64]{0,1:T(8,128)S(1)}, s32[]{:T(128)}) %tuple.34), condition=%wide.region_2.0_spmd, body=%wide.region_1.0_spmd.sunk | while | flops 201359360 | bytes 1966181 | solution.py:50
  104.4 3.4 %collective-permute-start = (f32[512,64]{0,1:T(8,128)S(1)}, f32[512,64]{0,1:T(8,128)S(1)}, u32[]{:S(2)}, u32[]{:S(2)}) collective-permute-start(f32[512,64]{0,1:T(8,128)S(1)} %convolution_add_fusion.5), channel_id=1, source_target_pairs={{0,1},{1,2},{2,3},{4,5},{5,6},{6,7},{8,9},{9,10},{10,11},{12,13},{... | collective-permute-start | bytes 393224 | tf_op jit(solution)/shard_map/while/body/eval_jaxpr/ppermute | solution.py:10
  107.8 2.6 %collective-permute-done = f32[512,64]{0,1:T(8,128)S(1)} collective-permute-done((f32[512,64]{0,1:T(8,128)S(1)}, f32[512,64]{0,1:T(8,128)S(1)}, u32[]{:S(2)}, u32[]{:S(2)}) %collective-permute-start) | collective-permute-done | bytes 131104 | tf_op jit(solution)/shard_map/while/body/eval_jaxpr/ppermute | solution.py:10
  111.5 4.4 %collective-permute-start = (f32[512,64]{0,1:T(8,128)S(1)}, f32[512,64]{0,1:T(8,128)S(1)}, u32[]{:S(2)}, u32[]{:S(2)}) collective-permute-start(f32[512,64]{0,1:T(8,128)S(1)} %convolution_add_fusion.5), channel_id=1, source_target_pairs={{0,1},{1,2},{2,3},{4,5},{5,6},{6,7},{8,9},{9,10},{10,11},{12,13},{... | collective-permute-start | bytes 393224 | tf_op jit(solution)/shard_map/while/body/eval_jaxpr/ppermute | solution.py:10
  119.5 4.4 %collective-permute-start = (f32[512,64]{0,1:T(8,128)S(1)}, f32[512,64]{0,1:T(8,128)S(1)}, u32[]{:S(2)}, u32[]{:S(2)}) collective-permute-start(f32[512,64]{0,1:T(8,128)S(1)} %convolution_add_fusion.5), channel_id=1, source_target_pairs={{0,1},{1,2},{2,3},{4,5},{5,6},{6,7},{8,9},{9,10},{10,11},{12,13},{... | collective-permute-start | bytes 393224 | tf_op jit(solution)/shard_map/while/body/eval_jaxpr/ppermute | solution.py:10
  129.1 24.6 %while.21 = (s32[]{:T(128)}, f32[512,64]{0,1:T(8,128)S(1)}, f32[512,512]{1,0:T(8,128)S(1)}, f32[512,64]{0,1:T(8,128)S(1)}, s32[]{:T(128)}) while((s32[]{:T(128)}, f32[512,64]{0,1:T(8,128)S(1)}, f32[512,512]{1,0:T(8,128)S(1)}, f32[512,64]{0,1:T(8,128)S(1)}, s32[]{:T(128)}) %tuple.37), condition=%wide.region_4.0_spmd, body=%wide.region_3.0_spmd.sunk | while | flops 201359360 | bytes 1966181 | solution.py:58
  131.5 6.0 %collective-permute-done.1 = f32[512,64]{0,1:T(8,128)S(1)} collective-permute-done((f32[512,64]{0,1:T(8,128)S(1)}, f32[512,64]{0,1:T(8,128)S(1)}, u32[]{:S(2)}, u32[]{:S(2)}) %collective-permute-start.1) | collective-permute-done | bytes 131104 | tf_op jit(solution)/shard_map/while/body/eval_jaxpr/ppermute | solution.py:10
  140.0 5.6 %collective-permute-done.1 = f32[512,64]{0,1:T(8,128)S(1)} collective-permute-done((f32[512,64]{0,1:T(8,128)S(1)}, f32[512,64]{0,1:T(8,128)S(1)}, u32[]{:S(2)}, u32[]{:S(2)}) %collective-permute-start.1) | collective-permute-done | bytes 131104 | tf_op jit(solution)/shard_map/while/body/eval_jaxpr/ppermute | solution.py:10
  148.0 5.7 %collective-permute-done.1 = f32[512,64]{0,1:T(8,128)S(1)} collective-permute-done((f32[512,64]{0,1:T(8,128)S(1)}, f32[512,64]{0,1:T(8,128)S(1)}, u32[]{:S(2)}, u32[]{:S(2)}) %collective-permute-start.1) | collective-permute-done | bytes 131104 | tf_op jit(solution)/shard_map/while/body/eval_jaxpr/ppermute | solution.py:10
  155.5 2.6 %collective-permute-start.3 = (f32[512,64]{0,1:T(8,128)S(1)}, f32[512,64]{0,1:T(8,128)S(1)}, u32[]{:S(2)}, u32[]{:S(2)}) collective-permute-start(f32[512,64]{0,1:T(8,128)S(1)} %get-tuple-element.76), channel_id=1, source_target_pairs={{0,28},{4,0},{8,4},{12,8},{16,12},{20,16},{24,20},{28,24},{1,29},{... | collective-permute-start | bytes 393224 | tf_op jit(solution)/shard_map/ppermute | solution.py:74
  158.2 3.2 %collective-permute-done.2 = f32[512,64]{0,1:T(8,128)S(1)} collective-permute-done((f32[512,64]{0,1:T(8,128)S(1)}, f32[512,64]{0,1:T(8,128)S(1)}, u32[]{:S(2)}, u32[]{:S(2)}) %collective-permute-start.2) | collective-permute-done | bytes 131104 | tf_op jit(solution)/shard_map/ppermute | solution.py:69
  161.4 2.6 %collective-permute-start.5 = (f32[512,64]{0,1:T(8,128)S(1)}, f32[512,64]{0,1:T(8,128)S(1)}, u32[]{:S(2)}, u32[]{:S(2)}) collective-permute-start(f32[512,64]{0,1:T(8,128)S(1)} %collective-permute-done.3), channel_id=1, source_target_pairs={{0,28},{4,0},{8,4},{12,8},{16,12},{20,16},{24,20},{28,24},{1,29},{... | collective-permute-start | bytes 393224 | tf_op jit(solution)/shard_map/ppermute | solution.py:74
  165.3 2.5 %collective-permute-done.4 = f32[512,64]{0,1:T(8,128)S(1)} collective-permute-done((f32[512,64]{0,1:T(8,128)S(1)}, f32[512,64]{0,1:T(8,128)S(1)}, u32[]{:S(2)}, u32[]{:S(2)}) %collective-permute-start.4) | collective-permute-done | bytes 131104 | tf_op jit(solution)/shard_map/ppermute | solution.py:69
  167.8 2.6 %collective-permute-start.7 = (f32[512,64]{0,1:T(8,128)S(1)}, f32[512,64]{0,1:T(8,128)S(1)}, u32[]{:S(2)}, u32[]{:S(2)}) collective-permute-start(f32[512,64]{0,1:T(8,128)S(1)} %collective-permute-done.5), channel_id=1, source_target_pairs={{0,28},{4,0},{8,4},{12,8},{16,12},{20,16},{24,20},{28,24},{1,29},{... | collective-permute-start | bytes 393224 | tf_op jit(solution)/shard_map/ppermute | solution.py:74
  175.5 4.0 %collective-permute-done.8 = f32[512,64]{0,1:T(8,128)S(1)} collective-permute-done((f32[512,64]{0,1:T(8,128)S(1)}, f32[512,64]{0,1:T(8,128)S(1)}, u32[]{:S(2)}, u32[]{:S(2)}) %collective-permute-start.8) | collective-permute-done | bytes 131104 | tf_op jit(solution)/shard_map/ppermute | solution.py:69
  180.1 9.2 %fusion.2 = f32[1024,512]{1,0:T(8,128)} fusion(f32[512,1024]{1,0:T(8,128)S(1)} %copy-done.2, f32[512,512]{0,1:T(8,128)} %constant_dynamic-update-slice_fusion), kind=kOutput, calls=%fused_computation.18 | convolution fusion | flops 3221225472 | bytes 5242880 | tf_op jit(solution)/shard_map/dot_general | solution.py:27
  189.4 43.4 %reduce-scatter.5.cloned.1.call-done = f32[256,512]{1,0:T(8,128)} async-done(((f32[1024,512]{1,0:T(8,128)}), f32[256,512]{1,0:T(8,128)}) %reduce-scatter.5.cloned.1.call-update) | async-done | bytes 524304 | tf_op jit(solution)/shard_map/reduce_scatter | solution.py:78
  (53 shorter events, 33.6 us)
Async XLA Ops:
  6.5 60.0 %copy-start = (f32[512,512]{1,0:T(8,128)S(1)}, f32[512,512]{1,0:T(8,128)}, u32[]{:S(2)}) copy-start(f32[512,512]{1,0:T(8,128)} %param.12) | copy-start | bytes 3145732
  6.5 51.1 %all-gather.2.cloned.1.call-start = ((), (), s32[]{:S(2)}) async-start(), calls=%async_computation.2 | async-start | bytes 2621440 | tf_op jit(solution)/shard_map/all_gather | solution.py:38
  7.3 93.9 %reduce-scatter.7.cloned.1.call-start = ((), (), s32[]{:S(2)}) async-start(), calls=%async_computation.4 | async-start | bytes 1179648
  18.0 45.7 %copy-start.1 = (f32[512,1024]{1,0:T(8,128)}, f32[512,1024]{1,0:T(8,128)S(1)}, u32[]{:S(2)}) copy-start(f32[512,1024]{1,0:T(8,128)S(1)} %mul.37) | copy-start | bytes 6291460
  66.3 166.5 %reduce-scatter.5.cloned.1.call-start = ((), (), s32[]{:S(2)}) async-start(), calls=%async_computation.3 | async-start | bytes 2621440 | tf_op jit(solution)/shard_map/reduce_scatter | solution.py:78
  104.4 6.0 %collective-permute-start = (f32[512,64]{0,1:T(8,128)S(1)}, f32[512,64]{0,1:T(8,128)S(1)}, u32[]{:S(2)}, u32[]{:S(2)}) collective-permute-start(f32[512,64]{0,1:T(8,128)S(1)} %convolution_add_fusion.5), channel_id=1, source_target_pairs={{0,1},{1,2},{2,3},{4,5},{5,6},{6,7},{8,9},{9,10},{10,11},{12,13},{... | collective-permute-start | bytes 393224 | tf_op jit(solution)/shard_map/while/body/eval_jaxpr/ppermute | solution.py:10
  111.5 6.9 %collective-permute-start = (f32[512,64]{0,1:T(8,128)S(1)}, f32[512,64]{0,1:T(8,128)S(1)}, u32[]{:S(2)}, u32[]{:S(2)}) collective-permute-start(f32[512,64]{0,1:T(8,128)S(1)} %convolution_add_fusion.5), channel_id=1, source_target_pairs={{0,1},{1,2},{2,3},{4,5},{5,6},{6,7},{8,9},{9,10},{10,11},{12,13},{... | collective-permute-start | bytes 393224 | tf_op jit(solution)/shard_map/while/body/eval_jaxpr/ppermute | solution.py:10
  119.5 6.9 %collective-permute-start = (f32[512,64]{0,1:T(8,128)S(1)}, f32[512,64]{0,1:T(8,128)S(1)}, u32[]{:S(2)}, u32[]{:S(2)}) collective-permute-start(f32[512,64]{0,1:T(8,128)S(1)} %convolution_add_fusion.5), channel_id=1, source_target_pairs={{0,1},{1,2},{2,3},{4,5},{5,6},{6,7},{8,9},{9,10},{10,11},{12,13},{... | collective-permute-start | bytes 393224 | tf_op jit(solution)/shard_map/while/body/eval_jaxpr/ppermute | solution.py:10
  126.4 1.9 copy-start.3
  130.2 7.3 %collective-permute-start.1 = (f32[512,64]{0,1:T(8,128)S(1)}, f32[512,64]{0,1:T(8,128)S(1)}, u32[]{:S(2)}, u32[]{:S(2)}) collective-permute-start(f32[512,64]{0,1:T(8,128)S(1)} %convolution_add_fusion.6), channel_id=1, source_target_pairs={{1,0},{2,1},{3,2},{5,4},{6,5},{7,6},{9,8},{10,9},{11,10},{13,12},{... | collective-permute-start | bytes 393224 | tf_op jit(solution)/shard_map/while/body/eval_jaxpr/ppermute | solution.py:10
  138.7 6.9 %collective-permute-start.1 = (f32[512,64]{0,1:T(8,128)S(1)}, f32[512,64]{0,1:T(8,128)S(1)}, u32[]{:S(2)}, u32[]{:S(2)}) collective-permute-start(f32[512,64]{0,1:T(8,128)S(1)} %convolution_add_fusion.6), channel_id=1, source_target_pairs={{1,0},{2,1},{3,2},{5,4},{6,5},{7,6},{9,8},{10,9},{11,10},{13,12},{... | collective-permute-start | bytes 393224 | tf_op jit(solution)/shard_map/while/body/eval_jaxpr/ppermute | solution.py:10
  146.7 7.0 %collective-permute-start.1 = (f32[512,64]{0,1:T(8,128)S(1)}, f32[512,64]{0,1:T(8,128)S(1)}, u32[]{:S(2)}, u32[]{:S(2)}) collective-permute-start(f32[512,64]{0,1:T(8,128)S(1)} %convolution_add_fusion.6), channel_id=1, source_target_pairs={{1,0},{2,1},{3,2},{5,4},{6,5},{7,6},{9,8},{10,9},{11,10},{13,12},{... | collective-permute-start | bytes 393224 | tf_op jit(solution)/shard_map/while/body/eval_jaxpr/ppermute | solution.py:10
  153.6 26.5 %copy-start.2 = (f32[512,1024]{1,0:T(8,128)S(1)}, f32[512,1024]{1,0:T(8,128)}, u32[]{:S(2)}) copy-start(f32[512,1024]{1,0:T(8,128)} %copy-done.1) | copy-start | bytes 6291460
  154.5 1.0 copy-start.4
  155.5 5.9 %collective-permute-start.2 = (f32[512,64]{0,1:T(8,128)S(1)}, f32[512,64]{0,1:T(8,128)S(1)}, u32[]{:S(2)}, u32[]{:S(2)}) collective-permute-start(f32[512,64]{0,1:T(8,128)S(1)} %get-tuple-element.76), channel_id=1, source_target_pairs={{0,4},{4,8},{8,12},{12,16},{16,20},{20,24},{24,28},{28,0},{1,5},{5... | collective-permute-start | bytes 393224 | tf_op jit(solution)/shard_map/ppermute | solution.py:69
  155.5 5.9 %collective-permute-start.3 = (f32[512,64]{0,1:T(8,128)S(1)}, f32[512,64]{0,1:T(8,128)S(1)}, u32[]{:S(2)}, u32[]{:S(2)}) collective-permute-start(f32[512,64]{0,1:T(8,128)S(1)} %get-tuple-element.76), channel_id=1, source_target_pairs={{0,28},{4,0},{8,4},{12,8},{16,12},{20,16},{24,20},{28,24},{1,29},{... | collective-permute-start | bytes 393224 | tf_op jit(solution)/shard_map/ppermute | solution.py:74
  161.4 6.5 %collective-permute-start.4 = (f32[512,64]{0,1:T(8,128)S(1)}, f32[512,64]{0,1:T(8,128)S(1)}, u32[]{:S(2)}, u32[]{:S(2)}) collective-permute-start(f32[512,64]{0,1:T(8,128)S(1)} %collective-permute-done.2), channel_id=1, source_target_pairs={{0,4},{4,8},{8,12},{12,16},{16,20},{20,24},{24,28},{28,0},{1,5},{5... | collective-permute-start | bytes 393224 | tf_op jit(solution)/shard_map/ppermute | solution.py:69
  161.4 6.5 %collective-permute-start.5 = (f32[512,64]{0,1:T(8,128)S(1)}, f32[512,64]{0,1:T(8,128)S(1)}, u32[]{:S(2)}, u32[]{:S(2)}) collective-permute-start(f32[512,64]{0,1:T(8,128)S(1)} %collective-permute-done.3), channel_id=1, source_target_pairs={{0,28},{4,0},{8,4},{12,8},{16,12},{20,16},{24,20},{28,24},{1,29},{... | collective-permute-start | bytes 393224 | tf_op jit(solution)/shard_map/ppermute | solution.py:74
  167.8 6.3 %collective-permute-start.6 = (f32[512,64]{0,1:T(8,128)S(1)}, f32[512,64]{0,1:T(8,128)S(1)}, u32[]{:S(2)}, u32[]{:S(2)}) collective-permute-start(f32[512,64]{0,1:T(8,128)S(1)} %collective-permute-done.4), channel_id=1, source_target_pairs={{0,4},{4,8},{8,12},{12,16},{16,20},{20,24},{24,28},{28,0},{1,5},{5... | collective-permute-start | bytes 393224 | tf_op jit(solution)/shard_map/ppermute | solution.py:69
  167.8 7.0 %collective-permute-start.7 = (f32[512,64]{0,1:T(8,128)S(1)}, f32[512,64]{0,1:T(8,128)S(1)}, u32[]{:S(2)}, u32[]{:S(2)}) collective-permute-start(f32[512,64]{0,1:T(8,128)S(1)} %collective-permute-done.5), channel_id=1, source_target_pairs={{0,28},{4,0},{8,4},{12,8},{16,12},{20,16},{24,20},{28,24},{1,29},{... | collective-permute-start | bytes 393224 | tf_op jit(solution)/shard_map/ppermute | solution.py:74
  174.2 5.3 %collective-permute-start.8 = (f32[512,64]{0,1:T(8,128)S(1)}, f32[512,64]{0,1:T(8,128)S(1)}, u32[]{:S(2)}, u32[]{:S(2)}) collective-permute-start(f32[512,64]{0,1:T(8,128)S(1)} %collective-permute-done.6), channel_id=1, source_target_pairs={{0,4},{4,8},{8,12},{12,16},{16,20},{20,24},{24,28},{28,0},{1,5},{5... | collective-permute-start | bytes 393224 | tf_op jit(solution)/shard_map/ppermute | solution.py:69
Sparse Core Ops, SparseCore 0:
  8.9 48.6 all-gather.1
  66.4 34.7 reduce-scatter.6
  189.5 43.2 reduce-scatter.4
